TPU v7x, 32 devices: a whole 2x2x4 slice. The times are simulated.
32 devices in a mesh: dp: 4 (over x, core), shard: 8 (over z, y).
Axes of the slice: x: 2, y: 2, z: 4, core: 2. Of those that a mesh axis runs over, the one named last changes fastest.
Arguments:
- tokens: bfloat16 [256, 6144], P('dp', 'shard'), may hold values from -6 to 6
- cotangent: bfloat16 [256, 6144], P('dp', 'shard'), may hold values from -12 to 12
- gate_proj: bfloat16 [2, 6144, 16384], P(None, 'dp', 'shard'), may hold values from -0.078125 to 0.078125
- up_proj: bfloat16 [2, 6144, 16384], P(None, 'dp', 'shard'), may hold values from -0.078125 to 0.078125
- down_proj: bfloat16 [2, 16384, 6144], P(None, 'shard', 'dp'), may hold values from -0.046875 to 0.046875
- slot_tokens: int32 [2, 64], P(None, 'dp'), may hold values from 0 to 63, as said below
- gate_weights: float32 [2, 64], P(None, 'dp'), may hold values from 0.1 to 1
- live_counts: int32 [2, 4], P(None, 'dp'), may hold values from 1 to 16, as said below
Outputs:
- grad_tokens: bfloat16 [256, 6144], P('dp', 'shard')
- grad_gate_proj: bfloat16 [2, 6144, 16384], P(None, 'dp', 'shard')
- grad_up_proj: bfloat16 [2, 6144, 16384], P(None, 'dp', 'shard')
- grad_down_proj: bfloat16 [2, 16384, 6144], P(None, 'shard', 'dp')
Inputs may be any that keep to these rules, and one draw needn't show every extreme that they name: `slot_tokens`: for each expert and each index of dp, the 16 slots name 16 different tokens of that index. `live_counts`: the live slots of an expert at an index of dp are its first ones; 16 is reached at some index of every expert.
All inputs are finite; a program needn't handle non-finite values.
Results may differ from a plain program's by a relative error of at most 0.03.
Values may be sent and summed in bfloat16 or wider, within the bound.
A program may use at most 128 MiB of HBM per device.

v0:
```python
import jax
import jax.numpy as jnp
from jax import lax
from jax.sharding import PartitionSpec as P


def slope_terms(gate_sum, up_sum, cot_hidden):
    sigmoid_part = jax.nn.sigmoid(gate_sum)
    grad_gate = (
        cot_hidden * up_sum * sigmoid_part * (1.0 + gate_sum * (1.0 - sigmoid_part))
    ).astype(jnp.bfloat16)
    grad_up = (cot_hidden * gate_sum * sigmoid_part).astype(jnp.bfloat16)
    return (grad_gate, grad_up)


def on_device(
    tokens, cotangent, gate_proj, up_proj, down_proj, slot_tokens, gate_weights, live_counts
):
    experts_here = slot_tokens.shape[0]
    slot_count = slot_tokens.shape[1]
    token_count = tokens.shape[0]
    position = lax.broadcasted_iota(jnp.int32, slot_tokens.shape, 1)
    alive_mask = (position < live_counts).astype(jnp.float32)
    picked = tokens[slot_tokens]
    weighted = (
        cotangent[slot_tokens].astype(jnp.float32) * (gate_weights * alive_mask)[:, :, None]
    ).astype(jnp.bfloat16)
    full_rows, full_cot = (
        lax.all_gather(picked, "shard", axis=2, tiled=True),
        lax.all_gather(weighted, "shard", axis=2, tiled=True),
    )
    block_rows, block_cot = (
        lax.all_to_all(full_rows, "dp", split_axis=2, concat_axis=1, tiled=True),
        lax.all_to_all(full_cot, "dp", split_axis=2, concat_axis=1, tiled=True),
    )
    totals = lax.psum(live_counts, "dp").astype(jnp.float32)
    gate_part = jnp.einsum(
        "erd,edf->erf", block_rows, gate_proj, preferred_element_type=jnp.float32
    )
    up_part = jnp.einsum("erd,edf->erf", block_rows, up_proj, preferred_element_type=jnp.float32)
    cot_part = jnp.einsum("erd,efd->erf", block_cot, down_proj, preferred_element_type=jnp.float32)
    gate_total, up_total = (
        lax.psum(gate_part.astype(jnp.bfloat16), "dp").astype(jnp.float32),
        lax.psum(up_part.astype(jnp.bfloat16), "dp").astype(jnp.float32),
    )
    hidden_all = (jax.nn.silu(gate_total) * up_total).astype(jnp.bfloat16)
    cot_total = lax.psum(cot_part.astype(jnp.bfloat16), "dp").astype(jnp.float32)
    gate_all, up_all = slope_terms(gate_total, up_total, cot_total)
    scale_back = totals[:, :, None]
    grad_down_proj = (
        jnp.einsum("erf,erd->efd", hidden_all, block_cot, preferred_element_type=jnp.float32)
        / scale_back
    ).astype(jnp.bfloat16)
    grad_gate_proj = (
        jnp.einsum("erd,erf->edf", block_rows, gate_all, preferred_element_type=jnp.float32)
        / scale_back
    ).astype(jnp.bfloat16)
    grad_up_proj = (
        jnp.einsum("erd,erf->edf", block_rows, up_all, preferred_element_type=jnp.float32)
        / scale_back
    ).astype(jnp.bfloat16)
    back_term = (
        jnp.einsum("erf,edf->erd", gate_all, gate_proj, preferred_element_type=jnp.float32)
        + jnp.einsum("erf,edf->erd", up_all, up_proj, preferred_element_type=jnp.float32)
    ).astype(jnp.bfloat16)
    owned_rows = lax.all_to_all(back_term, "dp", split_axis=1, concat_axis=2, tiled=True)
    row_grads = lax.psum_scatter(
        owned_rows.astype(jnp.float32).astype(jnp.bfloat16),
        "shard",
        scatter_dimension=2,
        tiled=True,
    ).astype(jnp.float32)
    one_hot = (
        slot_tokens[:, :, None]
        == lax.broadcasted_iota(jnp.int32, (experts_here, slot_count, token_count), 2)
    ).astype(jnp.float32)
    grad_tokens = jnp.einsum("ert,erf->tf", one_hot, row_grads).astype(jnp.bfloat16)
    return (grad_tokens, grad_gate_proj, grad_up_proj, grad_down_proj)


def solution(mesh):
    in_specs = (
        P("dp", "shard"),
        P("dp", "shard"),
        P(None, "dp", "shard"),
        P(None, "dp", "shard"),
        P(None, "shard", "dp"),
        P(None, "dp"),
        P(None, "dp"),
        P(None, "dp"),
    )
    out_specs = (
        P("dp", "shard"),
        P(None, "dp", "shard"),
        P(None, "dp", "shard"),
        P(None, "shard", "dp"),
    )
    return jax.shard_map(
        on_device, mesh=mesh, in_specs=in_specs, out_specs=out_specs, check_vma=False
    )
```

profile of v0, /device:TPU:0, one launch (start us, length us, event | category | flops | bytes accessed | tf_op | source)
XLA Modules:
  0.0 307.7 jit_solution(18017264233754935161)
XLA Ops:
  7.2 0.0 copy-start
  7.2 0.7 compare_select_fusion
  7.9 0.1 reshape.13
  8.0 0.1 copy-done
  8.1 0.6 gather_fusion.1
  8.7 34.9 %all-gather = bf16[2,16,6144]{2,1,0:T(8,128)(2,1)} all-gather(bf16[2,16,768]{2,1,0:T(8,128)(2,1)S(1)} %bitcast.48), channel_id=2, replica_groups=mesh['dp'=4,'shard'=8] {'shard'}, dimensions={2}, use_global_device_ids=true | all-gather | bytes 442368 | tf_op jit(solution)/shard_map/all_gather | solution.py:29
  43.6 6.1 %copy.27 = bf16[2,16,6144]{1,0,2:T(2,128)(2,1)S(1)} copy(bf16[2,16,6144]{2,1,0:T(8,128)(2,1)} %all-gather) | data formatting | bytes 786432 | tf_op jit(solution)/shard_map/all_gather | solution.py:29
  49.7 3.9 %reshape.34 = bf16[4,2,24576]{2,1,0:T(2,128)(2,1)} reshape(bf16[6144,2,16]{2,1,0:T(2,128)(2,1)S(1)} %bitcast.39) | data formatting | bytes 786432
  53.6 4.1 %all-to-all-start.1 = ((bf16[4,2,24576]{2,1,0:T(2,128)(2,1)}), bf16[4,2,24576]{2,1,0:T(2,128)(2,1)}, u32[]{:S(2)}, u32[]{:S(2)}) async-start(bf16[4,2,24576]{2,1,0:T(2,128)(2,1)} %reshape.34), calls=%async_computation.1 | async-start | bytes 786432 | tf_op jit(solution)/shard_map/all_to_all | solution.py:33
  57.7 1.6 gather_fusion
  59.3 0.8 compare_select_fusion.1
  60.0 0.1 fusion.14
  60.1 33.0 %all_gather.6 = bf16[2,16,6144]{2,1,0:T(8,128)(2,1)} all-gather(bf16[2,16,768]{2,1,0:T(8,128)(2,1)S(1)} %fusion.14), channel_id=1, replica_groups=mesh['dp'=4,'shard'=8] {'shard'}, dimensions={2}, use_global_device_ids=true | all-gather | bytes 442368 | tf_op jit(solution)/shard_map/all_gather | solution.py:30
  93.1 6.1 %copy.24 = bf16[2,16,6144]{1,0,2:T(2,128)(2,1)S(1)} copy(bf16[2,16,6144]{2,1,0:T(8,128)(2,1)} %all_gather.6) | data formatting | bytes 786432 | tf_op jit(solution)/shard_map/all_gather | solution.py:30
  99.2 3.9 %reshape.36 = bf16[4,2,24576]{2,1,0:T(2,128)(2,1)} reshape(bf16[6144,2,16]{2,1,0:T(2,128)(2,1)S(1)} %bitcast.40) | data formatting | bytes 786432
  103.1 0.0 all-to-all-done.1
  103.1 4.1 %all-to-all-start = ((bf16[4,2,24576]{2,1,0:T(2,128)(2,1)}), bf16[4,2,24576]{2,1,0:T(2,128)(2,1)}, u32[]{:S(2)}, u32[]{:S(2)}) async-start(bf16[4,2,24576]{2,1,0:T(2,128)(2,1)} %reshape.36), calls=%async_computation | async-start | bytes 786432 | tf_op jit(solution)/shard_map/all_to_all | solution.py:34
  107.2 0.0 all-reduce.3.cloned.1.call-start
  107.2 3.5 %reshape.35 = bf16[6144,2,16]{2,1,0:T(2,128)(2,1)S(1)} reshape(bf16[4,2,24576]{2,1,0:T(2,128)(2,1)} %all-to-all-done.1) | data formatting | bytes 786432
  110.7 4.8 %copy.33 = bf16[2,16,4,1536]{3,2,1,0:T(4,128)(2,1)} copy(bf16[2,16,4,1536]{1,0,3,2:T(2,128)(2,1)S(1)} %bitcast.41) | data formatting | bytes 786432 | tf_op jit(solution)/shard_map/all_to_all | solution.py:33
  115.6 1.1 copy.29
  116.6 7.7 %convolution_convert_fusion = bf16[2,64,2048]{2,1,0:T(8,128)(2,1)} fusion(bf16[2,64,1536]{2,1,0:T(8,128)(2,1)S(1)} %bitcast.35, bf16[2,1536,2048]{2,1,0:T(8,128)(2,1)} %param.10), kind=kOutput, calls=%fused_computation.6 | convolution fusion | flops 805568512 | bytes 13500416 | tf_op jit(solution)/shard_map/erd,edf->erf/dot_general | solution.py:37
  124.3 7.7 %convolution_convert_fusion.1 = bf16[2,64,2048]{2,1,0:T(8,128)(2,1)} fusion(bf16[2,64,1536]{2,1,0:T(8,128)(2,1)S(1)} %bitcast.36, bf16[2,1536,2048]{2,1,0:T(8,128)(2,1)} %param.11), kind=kOutput, calls=%fused_computation.7 | convolution fusion | flops 805568512 | bytes 13500416 | tf_op jit(solution)/shard_map/erd,edf->erf/dot_general | solution.py:40
  132.0 0.0 copy-start.3
  132.0 0.0 all-to-all-done
  132.0 4.7 %reshape.37 = bf16[6144,2,16]{2,1,0:T(2,128)(2,1)} reshape(bf16[4,2,24576]{2,1,0:T(2,128)(2,1)} %all-to-all-done) | data formatting | bytes 786432
  136.7 7.3 %copy.32 = bf16[2,16,4,1536]{3,2,1,0:T(4,128)(2,1)S(1)} copy(bf16[2,16,4,1536]{1,0,3,2:T(2,128)(2,1)} %bitcast.42) | data formatting | bytes 786432 | tf_op jit(solution)/shard_map/all_to_all | solution.py:34
  144.0 0.1 copy.26
  144.0 9.2 %convolution_convert_fusion.2 = bf16[2,64,2048]{2,1,0:T(8,128)(2,1)} fusion(bf16[2,64,1536]{2,1,0:T(8,128)(2,1)S(1)} %bitcast.43, bf16[2,2048,1536]{2,1,0:T(8,128)(2,1)} %param.12), kind=kOutput, calls=%fused_computation.8 | convolution fusion | flops 805568512 | bytes 13500416 | tf_op jit(solution)/shard_map/erd,efd->erf/dot_general | solution.py:41
  153.3 0.0 all-reduce.3.cloned.1.call-update
  153.3 0.0 copy-done.3
  153.3 5.6 %psum.31 = s32[2,1]{0,1:T(1,128)S(1)} all-reduce(s32[2,1]{0,1:T(1,128)S(1)} %copy-done.3), channel_id=1, replica_groups=mesh['dp'=4,'shard'=8] {'dp'}, use_global_device_ids=true, to_apply=%region_4.5 | all-reduce | flops 2 | bytes 16 | tf_op jit(solution)/shard_map/psum | solution.py:36
  158.9 39.1 %all-reduce.3.cloned.1.call-done = (bf16[2,64,2048]{2,1,0:T(8,128)(2,1)}, bf16[2,64,2048]{2,1,0:T(8,128)(2,1)}, bf16[2,64,2048]{2,1,0:T(8,128)(2,1)}) async-done(((bf16[2,64,2048]{2,1,0:T(8,128)(2,1)}, bf16[2,64,2048]{2,1,0:T(8,128)(2,1)}, bf16[2,64,2048]{2,1,0:T(8,128)(2,1)}), (bf16[2,64,2048]{2,1,0:T(8,128)(2,1)}, bf16[2,64,2048]{2,1,0:T(8,128)(2,1)}, ...) | async-done | bytes 1572880 | tf_op jit(solution)/shard_map/psum | solution.py:44
  198.0 0.0 copy-start.4
  198.0 0.0 copy-start.5
  198.0 9.1 %fusion.20 = f32[2,64,1536]{2,1,0:T(8,128)S(1)} fusion(bf16[2,1536,2048]{2,1,0:T(8,128)(2,1)} %param.10, bf16[2,64,2048]{2,1,0:T(8,128)(2,1)} %get-tuple-element.4, bf16[2,64,2048]{2,1,0:T(8,128)(2,1)} %get-tuple-element.5, bf16[2,64,2048]{2,1,0:T(8,128)(2,1)} %get-tuple-element.6), kind=kOutput, calls=%fused_computation.38 | convolution fusion | flops 808714240 | bytes 14942208 | tf_op jit(solution)/shard_map/erf,edf->erd/dot_general | solution.py:63
  207.1 0.0 copy-done.4
  207.1 0.0 copy-done.5
  207.1 0.0 copy-start.6
  207.1 8.6 %fusion = bf16[2,64,1536]{2,1,0:T(8,128)(2,1)S(1)} fusion(f32[2,64,1536]{2,1,0:T(8,128)S(1)} %fusion.20, bf16[2,1536,2048]{2,1,0:T(8,128)(2,1)} %param.11, bf16[2,64,2048]{2,1,0:T(8,128)(2,1)S(1)} %copy-done.5, bf16[2,64,2048]{2,1,0:T(8,128)(2,1)S(1)} %copy-done.4), kind=kOutput, calls=%fused_computation.9 | convolution fusion | flops 807796736 | bytes 14811136 | tf_op jit(solution)/shard_map/erf,edf->erd/dot_general | solution.py:64
  215.7 1.2 copy.30
  216.8 3.5 %all-to-all-start.2 = ((bf16[2,64,1536]{2,0,1:T(2,128)(2,1)}), bf16[2,64,1536]{2,0,1:T(2,128)(2,1)S(1)}, u32[]{:S(2)}, u32[]{:S(2)}) async-start(bf16[2,64,1536]{2,0,1:T(2,128)(2,1)} %copy.30), calls=%async_computation.2 | async-start | bytes 786432 | tf_op jit(solution)/shard_map/all_to_all | solution.py:66
  220.3 0.3 reduce-scatter.2.cloned.1.call-start
  220.5 0.0 copy-done.6
  220.6 6.7 %divide_convert_fusion.2 = bf16[2,1536,2048]{2,1,0:T(8,128)(2,1)} fusion(f32[2]{0:T(128)S(1)} %convert_bitcast_fusion, bf16[2,64,1536]{2,1,0:T(8,128)(2,1)S(1)} %bitcast.37, bf16[2,64,2048]{2,1,0:T(8,128)(2,1)S(1)} %copy-done.6, bf16[2,64,2048]{2,1,0:T(8,128)(2,1)S(1)} %copy-done.4, bf16[2,64,2048]{2,1,0:T(8,128)(2,1)S(1)} %copy-done.5), kind=kOutput, calls=%fused_computation.4 | convolution fusion | flops 821297152 | bytes 14549000 | tf_op jit(solution)/shard_map/erd,erf->edf/dot_general | solution.py:55
  227.3 6.9 %divide_convert_fusion = bf16[2,2048,1536]{2,1,0:T(8,128)(2,1)} fusion(f32[2]{0:T(128)S(1)} %convert_bitcast_fusion, bf16[2,64,1536]{2,1,0:T(8,128)(2,1)S(1)} %bitcast.44, bf16[2,64,2048]{2,1,0:T(8,128)(2,1)S(1)} %copy-done.6, bf16[2,64,2048]{2,1,0:T(8,128)(2,1)S(1)} %copy-done.5), kind=kOutput, calls=%fused_computation.2 | convolution fusion | flops 819986432 | bytes 14024712 | tf_op jit(solution)/shard_map/erf,erd->efd/dot_general | solution.py:51
  234.2 0.0 all-to-all-done.2
  234.2 0.3 copy.31
  234.5 1.0 all_to_all.50
  235.5 0.0 reduce-scatter.2.cloned.1.call-update
  235.5 0.0 copy-start.2
  235.5 0.0 copy-start.1
  235.6 6.7 %divide_convert_fusion.1 = bf16[2,1536,2048]{2,1,0:T(8,128)(2,1)} fusion(f32[2]{0:T(128)S(1)} %convert_bitcast_fusion, bf16[2,64,1536]{2,1,0:T(8,128)(2,1)S(1)} %bitcast.38, bf16[2,64,2048]{2,1,0:T(8,128)(2,1)S(1)} %copy-done.5, bf16[2,64,2048]{2,1,0:T(8,128)(2,1)S(1)} %copy-done.4), kind=kOutput, calls=%fused_computation.3 | convolution fusion | flops 819986432 | bytes 14024712 | tf_op jit(solution)/shard_map/erd,erf->edf/dot_general | solution.py:59
  242.3 56.8 %reduce-scatter.2.cloned.1.call-done = bf16[2,16,768]{2,1,0:T(8,128)(2,1)} async-done(((bf16[2,16,6144]{2,1,0:T(8,128)(2,1)}), bf16[2,16,768]{2,1,0:T(8,128)(2,1)}) %reduce-scatter.2.cloned.1.call-update) | async-done | bytes 49168 | tf_op jit(solution)/shard_map/reduce_scatter | solution.py:67
  299.1 0.0 copy-done.2
  299.1 1.7 fusion.1
  300.8 0.0 copy-done.1
  (2 shorter events, 0.0 us)
Async XLA Ops:
  7.2 0.9 copy-start
  53.6 49.5 %all-to-all-start.1 = ((bf16[4,2,24576]{2,1,0:T(2,128)(2,1)}), bf16[4,2,24576]{2,1,0:T(2,128)(2,1)}, u32[]{:S(2)}, u32[]{:S(2)}) async-start(bf16[4,2,24576]{2,1,0:T(2,128)(2,1)} %reshape.34), calls=%async_computation.1 | async-start | bytes 786432 | tf_op jit(solution)/shard_map/all_to_all | solution.py:33
  103.1 28.9 %all-to-all-start = ((bf16[4,2,24576]{2,1,0:T(2,128)(2,1)}), bf16[4,2,24576]{2,1,0:T(2,128)(2,1)}, u32[]{:S(2)}, u32[]{:S(2)}) async-start(bf16[4,2,24576]{2,1,0:T(2,128)(2,1)} %reshape.36), calls=%async_computation | async-start | bytes 786432 | tf_op jit(solution)/shard_map/all_to_all | solution.py:34
  107.2 90.8 %all-reduce.3.cloned.1.call-start = ((), (), s32[]{:S(2)}) async-start(), calls=%async_computation.5 | async-start | bytes 3145728 | tf_op jit(solution)/shard_map/psum | solution.py:44
  132.0 21.3 %copy-start.3 = (s32[2,1]{0,1:T(1,128)S(1)}, s32[2,1]{0,1:T(1,128)}, u32[]{:S(2)}) copy-start(s32[2,1]{0,1:T(1,128)} %param.15) | copy-start | bytes 28
  198.0 9.1 %copy-start.4 = (bf16[2,64,2048]{2,1,0:T(8,128)(2,1)S(1)}, bf16[2,64,2048]{2,1,0:T(8,128)(2,1)}, u32[]{:S(2)}) copy-start(bf16[2,64,2048]{2,1,0:T(8,128)(2,1)} %get-tuple-element.5) | copy-start | bytes 1572868
  198.0 9.1 %copy-start.5 = (bf16[2,64,2048]{2,1,0:T(8,128)(2,1)S(1)}, bf16[2,64,2048]{2,1,0:T(8,128)(2,1)}, u32[]{:S(2)}) copy-start(bf16[2,64,2048]{2,1,0:T(8,128)(2,1)} %get-tuple-element.6) | copy-start | bytes 1572868
  207.1 13.5 %copy-start.6 = (bf16[2,64,2048]{2,1,0:T(8,128)(2,1)S(1)}, bf16[2,64,2048]{2,1,0:T(8,128)(2,1)}, u32[]{:S(2)}) copy-start(bf16[2,64,2048]{2,1,0:T(8,128)(2,1)} %get-tuple-element.4) | copy-start | bytes 1572868
  216.8 17.4 %all-to-all-start.2 = ((bf16[2,64,1536]{2,0,1:T(2,128)(2,1)}), bf16[2,64,1536]{2,0,1:T(2,128)(2,1)S(1)}, u32[]{:S(2)}, u32[]{:S(2)}) async-start(bf16[2,64,1536]{2,0,1:T(2,128)(2,1)} %copy.30), calls=%async_computation.2 | async-start | bytes 786432 | tf_op jit(solution)/shard_map/all_to_all | solution.py:66
  220.3 78.8 %reduce-scatter.2.cloned.1.call-start = ((), (), s32[]{:S(2)}) async-start(), calls=%async_computation.4 | async-start | bytes 442368 | tf_op jit(solution)/shard_map/reduce_scatter | solution.py:67
  235.5 63.6 %copy-start.2 = (s32[2,16]{1,0:T(2,128)S(1)}, s32[2,16]{1,0:T(2,128)}, u32[]{:S(2)}) copy-start(s32[2,16]{1,0:T(2,128)} %param.13) | copy-start | bytes 388
  235.5 65.3 %copy-start.1 = (bf16[64,768]{1,0:T(8,128)(2,1)S(1)}, bf16[64,768]{1,0:T(8,128)(2,1)}, u32[]{:S(2)}) copy-start(bf16[64,768]{1,0:T(8,128)(2,1)} %param.8) | copy-start | bytes 294916
Sparse Core Ops, SparseCore 0:
  153.4 44.5 all-reduce.2
  235.7 63.4 reduce-scatter.1
where the time goes:
time: 309 us; the launch traced here: 308 us
  waiting for transfers between devices  96 us (31%)
  blocking collectives  73.4 us (24%)
  matrix products  64.3 us (21%)
  local copies, waits for them, and re-layouts  46.3 us (15%)
  between operations  14.2 us (5%)
  starting transfers between devices  12 us (4%)
    reduce_scatter x1, waiting for transfers between devices, on_device(): lax.psum_scatter(owned_rows.astype(jnp.float32).astype(jnp.bfloat16), 'sh...  56.8 us
    psum x1, waiting for transfers between devices, on_device(): lax.psum(up_part.astype(jnp.bfloat16), 'dp').astype(jnp.float32)  39.1 us
    all_gather x1, blocking collectives, on_device(): lax.all_gather(picked, 'shard', axis=2, tiled=True)  34.9 us
    all_gather x1, blocking collectives, on_device(): lax.all_gather(weighted, 'shard', axis=2, tiled=True)  33 us
    unnamed x18, local copies, waits for them, and re-layouts  16.1 us
    dot_general x1, matrix products, on_device(): jnp.einsum('erd,efd->erf', block_cot, down_proj, preferred_element_type=j...  9.24 us
    dot_general x1, matrix products, on_device(): jnp.einsum('erf,edf->erd', gate_all, gate_proj, preferred_element_type=jn...  9.06 us
    dot_general x1, matrix products, on_device(): jnp.einsum('erf,edf->erd', up_all, up_proj, preferred_element_type=jnp.fl...  8.55 us
  transfers between devices with their start and end apart: 5, of which 2 were waited for; matrix products, arithmetic and copies ran while one was open for 19% of the time, Pallas kernels for 0%

commit v1 on v0

--- a/solution.py
+++ b/solution.py
@@ -27,7 +27,7 @@
     ).astype(jnp.bfloat16)
     full_rows, full_cot = (
         lax.all_gather(picked, "shard", axis=2, tiled=True),
-        lax.all_gather(weighted, "shard", axis=2, tiled=True),
+        jnp.concatenate(lax.all_gather(weighted, "shard"), axis=2),
     )
     block_rows, block_cot = (
         lax.all_to_all(full_rows, "dp", split_axis=2, concat_axis=1, tiled=True),

time: 309 us -> 305 us (0.987)
  blocking collectives: 73.4 us -> 69.4 us
    all_gather x1 -> x0, local copies, waits for them, and re-layouts: 6.1 us -> none  [on_device(): lax.all_gather(weighted, 'shard', axis=2, tiled=True)]
    reshape x0 -> x1, local copies, waits for them, and re-layouts: none -> 5.43 us  [on_device(): jnp.concatenate(lax.all_gather(weighted, 'shard'), axis=2)]
  transfers between devices with their start and end apart: 5 -> 5, of which waited for: 2 -> 2; matrix products, arithmetic and copies ran while one was open for 19% -> 20% of each run, Pallas kernels for 0% -> 0%
where the time goes in v1:
time: 305 us; the launch traced here: 304 us
  waiting for transfers between devices  95.8 us (31%)
  blocking collectives  69.4 us (23%)
  matrix products  64.3 us (21%)
  local copies, waits for them, and re-layouts  47.7 us (16%)
  between operations  14.2 us (5%)
  starting transfers between devices  10.7 us (4%)
    reduce_scatter x1, waiting for transfers between devices, on_device(): lax.psum_scatter(owned_rows.astype(jnp.float32).astype(jnp.bfloat16), 'sh...  56.8 us
    psum x1, waiting for transfers between devices, on_device(): lax.psum(up_part.astype(jnp.bfloat16), 'dp').astype(jnp.float32)  38.9 us
    all_gather x1, blocking collectives, on_device(): lax.all_gather(picked, 'shard', axis=2, tiled=True)  32.8 us
    all_gather x1, blocking collectives, on_device(): lax.all_gather(weighted, 'shard')  31 us
    unnamed x18, local copies, waits for them, and re-layouts  17.8 us
    dot_general x1, matrix products, on_device(): jnp.einsum('erd,efd->erf', block_cot, down_proj, preferred_element_type=j...  9.24 us
    dot_general x1, matrix products, on_device(): jnp.einsum('erf,edf->erd', gate_all, gate_proj, preferred_element_type=jn...  9.06 us
    dot_general x1, matrix products, on_device(): jnp.einsum('erf,edf->erd', up_all, up_proj, preferred_element_type=jnp.fl...  8.55 us
  transfers between devices with their start and end apart: 5, of which 2 were waited for; matrix products, arithmetic and copies ran while one was open for 20% of the time, Pallas kernels for 0%

profile of v1, /device:TPU:0, one launch (start us, length us, event | category | flops | bytes accessed | tf_op | source)
XLA Modules:
  0.0 303.6 jit_solution(1542758554800516065)
XLA Ops:
  7.2 0.0 copy-start
  7.2 0.7 compare_select_fusion
  7.9 0.1 reshape.37
  8.0 0.1 copy-done
  8.1 0.6 gather_fusion.1
  8.7 32.8 %all-gather = bf16[2,16,6144]{2,1,0:T(8,128)(2,1)S(1)} all-gather(bf16[2,16,768]{2,1,0:T(8,128)(2,1)S(1)} %bitcast.51), channel_id=2, replica_groups=mesh['dp'=4,'shard'=8] {'shard'}, dimensions={2}, use_global_device_ids=true | all-gather | bytes 442368 | tf_op jit(solution)/shard_map/all_gather | solution.py:29
  41.5 5.0 %copy.30 = bf16[2,16,6144]{1,0,2:T(2,128)(2,1)} copy(bf16[2,16,6144]{2,1,0:T(8,128)(2,1)S(1)} %all-gather) | data formatting | bytes 786432 | tf_op jit(solution)/shard_map/all_gather | solution.py:29
  46.5 5.4 %reshape.59 = bf16[4,2,24576]{2,1,0:T(2,128)(2,1)} reshape(bf16[6144,2,16]{2,1,0:T(2,128)(2,1)} %bitcast.41) | data formatting | bytes 786432
  51.9 3.5 %all-to-all-start.1 = ((bf16[4,2,24576]{2,1,0:T(2,128)(2,1)}), bf16[4,2,24576]{2,1,0:T(2,128)(2,1)S(1)}, u32[]{:S(2)}, u32[]{:S(2)}) async-start(bf16[4,2,24576]{2,1,0:T(2,128)(2,1)} %reshape.59), calls=%async_computation.1 | async-start | bytes 786432 | tf_op jit(solution)/shard_map/all_to_all | solution.py:33
  55.4 1.6 gather_fusion
  57.0 0.8 compare_select_fusion.1
  57.7 0.1 fusion.14
  57.8 31.0 %all_gather.7 = bf16[8,2,16,768]{3,2,1,0:T(8,128)(2,1)S(1)} all-gather(bf16[1,2,16,768]{3,2,1,0:T(8,128)(2,1)S(1)} %fusion.14), channel_id=1, replica_groups=mesh['dp'=4,'shard'=8] {'shard'}, dimensions={0}, use_global_device_ids=true | all-gather | bytes 442368 | tf_op jit(solution)/shard_map/all_gather | solution.py:30
  88.7 5.4 %copy.35 = bf16[2,16,8,768]{1,0,3,2:T(2,128)(2,1)} copy(bf16[2,16,8,768]{3,1,0,2:T(8,128)(2,1)S(1)} %bitcast.48) | data formatting | bytes 786432 | tf_op jit(solution)/shard_map/reshape | solution.py:30
  94.2 5.4 %reshape.61 = bf16[4,2,24576]{2,1,0:T(2,128)(2,1)} reshape(bf16[6144,2,16]{2,1,0:T(2,128)(2,1)} %bitcast.42) | data formatting | bytes 786432
  99.6 0.0 all-to-all-done.1
  99.6 3.5 %all-to-all-start = ((bf16[4,2,24576]{2,1,0:T(2,128)(2,1)}), bf16[4,2,24576]{2,1,0:T(2,128)(2,1)S(1)}, u32[]{:S(2)}, u32[]{:S(2)}) async-start(bf16[4,2,24576]{2,1,0:T(2,128)(2,1)} %reshape.61), calls=%async_computation | async-start | bytes 786432 | tf_op jit(solution)/shard_map/all_to_all | solution.py:34
  103.1 0.0 all-reduce.3.cloned.1.call-start
  103.1 3.4 %reshape.60 = bf16[6144,2,16]{2,1,0:T(2,128)(2,1)} reshape(bf16[4,2,24576]{2,1,0:T(2,128)(2,1)S(1)} %all-to-all-done.1) | data formatting | bytes 786432
  106.5 7.3 %copy.37 = bf16[2,16,4,1536]{3,2,1,0:T(4,128)(2,1)S(1)} copy(bf16[2,16,4,1536]{1,0,3,2:T(2,128)(2,1)} %bitcast.43) | data formatting | bytes 786432 | tf_op jit(solution)/shard_map/all_to_all | solution.py:33
  113.8 0.1 copy.32
  113.9 7.7 %convolution_convert_fusion = bf16[2,64,2048]{2,1,0:T(8,128)(2,1)} fusion(bf16[2,64,1536]{2,1,0:T(8,128)(2,1)S(1)} %bitcast.37, bf16[2,1536,2048]{2,1,0:T(8,128)(2,1)} %param.10), kind=kOutput, calls=%fused_computation.6 | convolution fusion | flops 805568512 | bytes 13500416 | tf_op jit(solution)/shard_map/erd,edf->erf/dot_general | solution.py:37
  121.6 7.7 %convolution_convert_fusion.1 = bf16[2,64,2048]{2,1,0:T(8,128)(2,1)} fusion(bf16[2,64,1536]{2,1,0:T(8,128)(2,1)S(1)} %bitcast.38, bf16[2,1536,2048]{2,1,0:T(8,128)(2,1)} %param.11), kind=kOutput, calls=%fused_computation.7 | convolution fusion | flops 805568512 | bytes 13500416 | tf_op jit(solution)/shard_map/erd,edf->erf/dot_general | solution.py:40
  129.2 0.0 copy-start.3
  129.2 0.0 all-to-all-done
  129.2 3.4 %reshape.62 = bf16[6144,2,16]{2,1,0:T(2,128)(2,1)} reshape(bf16[4,2,24576]{2,1,0:T(2,128)(2,1)S(1)} %all-to-all-done) | data formatting | bytes 786432
  132.6 7.3 %copy.36 = bf16[2,16,4,1536]{3,2,1,0:T(4,128)(2,1)S(1)} copy(bf16[2,16,4,1536]{1,0,3,2:T(2,128)(2,1)} %bitcast.44) | data formatting | bytes 786432 | tf_op jit(solution)/shard_map/all_to_all | solution.py:34
  139.9 0.1 copy.29
  140.0 9.2 %convolution_convert_fusion.2 = bf16[2,64,2048]{2,1,0:T(8,128)(2,1)} fusion(bf16[2,64,1536]{2,1,0:T(8,128)(2,1)S(1)} %bitcast.45, bf16[2,2048,1536]{2,1,0:T(8,128)(2,1)} %param.12), kind=kOutput, calls=%fused_computation.8 | convolution fusion | flops 805568512 | bytes 13500416 | tf_op jit(solution)/shard_map/erd,efd->erf/dot_general | solution.py:41
  149.3 0.0 all-reduce.3.cloned.1.call-update
  149.3 0.0 copy-done.3
  149.3 5.7 %psum.31 = s32[2,1]{0,1:T(1,128)S(1)} all-reduce(s32[2,1]{0,1:T(1,128)S(1)} %copy-done.3), channel_id=1, replica_groups=mesh['dp'=4,'shard'=8] {'dp'}, use_global_device_ids=true, to_apply=%region_4.5 | all-reduce | flops 2 | bytes 16 | tf_op jit(solution)/shard_map/psum | solution.py:36
  155.0 38.9 %all-reduce.3.cloned.1.call-done = (bf16[2,64,2048]{2,1,0:T(8,128)(2,1)}, bf16[2,64,2048]{2,1,0:T(8,128)(2,1)}, bf16[2,64,2048]{2,1,0:T(8,128)(2,1)}) async-done(((bf16[2,64,2048]{2,1,0:T(8,128)(2,1)}, bf16[2,64,2048]{2,1,0:T(8,128)(2,1)}, bf16[2,64,2048]{2,1,0:T(8,128)(2,1)}), (bf16[2,64,2048]{2,1,0:T(8,128)(2,1)}, bf16[2,64,2048]{2,1,0:T(8,128)(2,1)}, ...) | async-done | bytes 1572880 | tf_op jit(solution)/shard_map/psum | solution.py:44
  193.9 0.0 copy-start.4
  193.9 0.0 copy-start.5
  193.9 9.1 %fusion.20 = f32[2,64,1536]{2,1,0:T(8,128)S(1)} fusion(bf16[2,1536,2048]{2,1,0:T(8,128)(2,1)} %param.10, bf16[2,64,2048]{2,1,0:T(8,128)(2,1)} %get-tuple-element.4, bf16[2,64,2048]{2,1,0:T(8,128)(2,1)} %get-tuple-element.5, bf16[2,64,2048]{2,1,0:T(8,128)(2,1)} %get-tuple-element.6), kind=kOutput, calls=%fused_computation.38 | convolution fusion | flops 808714240 | bytes 14942208 | tf_op jit(solution)/shard_map/erf,edf->erd/dot_general | solution.py:63
  203.0 0.0 copy-done.4
  203.0 0.0 copy-done.5
  203.0 0.0 copy-start.6
  203.0 8.6 %fusion = bf16[2,64,1536]{2,1,0:T(8,128)(2,1)S(1)} fusion(f32[2,64,1536]{2,1,0:T(8,128)S(1)} %fusion.20, bf16[2,1536,2048]{2,1,0:T(8,128)(2,1)} %param.11, bf16[2,64,2048]{2,1,0:T(8,128)(2,1)S(1)} %copy-done.5, bf16[2,64,2048]{2,1,0:T(8,128)(2,1)S(1)} %copy-done.4), kind=kOutput, calls=%fused_computation.9 | convolution fusion | flops 807796736 | bytes 14811136 | tf_op jit(solution)/shard_map/erf,edf->erd/dot_general | solution.py:64
  211.6 1.2 copy.33
  212.7 3.5 %all-to-all-start.2 = ((bf16[2,64,1536]{2,0,1:T(2,128)(2,1)}), bf16[2,64,1536]{2,0,1:T(2,128)(2,1)S(1)}, u32[]{:S(2)}, u32[]{:S(2)}) async-start(bf16[2,64,1536]{2,0,1:T(2,128)(2,1)} %copy.33), calls=%async_computation.2 | async-start | bytes 786432 | tf_op jit(solution)/shard_map/all_to_all | solution.py:66
  216.2 0.3 reduce-scatter.2.cloned.1.call-start
  216.4 0.0 copy-done.6
  216.5 6.7 %divide_convert_fusion.2 = bf16[2,1536,2048]{2,1,0:T(8,128)(2,1)} fusion(f32[2]{0:T(128)S(1)} %convert_bitcast_fusion, bf16[2,64,1536]{2,1,0:T(8,128)(2,1)S(1)} %bitcast.39, bf16[2,64,2048]{2,1,0:T(8,128)(2,1)S(1)} %copy-done.6, bf16[2,64,2048]{2,1,0:T(8,128)(2,1)S(1)} %copy-done.4, bf16[2,64,2048]{2,1,0:T(8,128)(2,1)S(1)} %copy-done.5), kind=kOutput, calls=%fused_computation.4 | convolution fusion | flops 821297152 | bytes 14549000 | tf_op jit(solution)/shard_map/erd,erf->edf/dot_general | solution.py:55
  223.2 6.9 %divide_convert_fusion = bf16[2,2048,1536]{2,1,0:T(8,128)(2,1)} fusion(f32[2]{0:T(128)S(1)} %convert_bitcast_fusion, bf16[2,64,1536]{2,1,0:T(8,128)(2,1)S(1)} %bitcast.46, bf16[2,64,2048]{2,1,0:T(8,128)(2,1)S(1)} %copy-done.6, bf16[2,64,2048]{2,1,0:T(8,128)(2,1)S(1)} %copy-done.5), kind=kOutput, calls=%fused_computation.2 | convolution fusion | flops 819986432 | bytes 14024712 | tf_op jit(solution)/shard_map/erf,erd->efd/dot_general | solution.py:51
  230.1 0.0 all-to-all-done.2
  230.1 0.3 copy.34
  230.4 1.0 all_to_all.50
  231.4 0.0 reduce-scatter.2.cloned.1.call-update
  231.4 0.0 copy-start.2
  231.4 0.0 copy-start.1
  231.5 6.7 %divide_convert_fusion.1 = bf16[2,1536,2048]{2,1,0:T(8,128)(2,1)} fusion(f32[2]{0:T(128)S(1)} %convert_bitcast_fusion, bf16[2,64,1536]{2,1,0:T(8,128)(2,1)S(1)} %bitcast.40, bf16[2,64,2048]{2,1,0:T(8,128)(2,1)S(1)} %copy-done.5, bf16[2,64,2048]{2,1,0:T(8,128)(2,1)S(1)} %copy-done.4), kind=kOutput, calls=%fused_computation.3 | convolution fusion | flops 819986432 | bytes 14024712 | tf_op jit(solution)/shard_map/erd,erf->edf/dot_general | solution.py:59
  238.2 56.8 %reduce-scatter.2.cloned.1.call-done = bf16[2,16,768]{2,1,0:T(8,128)(2,1)} async-done(((bf16[2,16,6144]{2,1,0:T(8,128)(2,1)}), bf16[2,16,768]{2,1,0:T(8,128)(2,1)}) %reduce-scatter.2.cloned.1.call-update) | async-done | bytes 49168 | tf_op jit(solution)/shard_map/reduce_scatter | solution.py:67
  295.0 0.0 copy-done.2
  295.0 1.7 fusion.1
  296.7 0.0 copy-done.1
  (2 shorter events, 0.0 us)
Async XLA Ops:
  7.2 0.9 copy-start
  51.9 47.7 %all-to-all-start.1 = ((bf16[4,2,24576]{2,1,0:T(2,128)(2,1)}), bf16[4,2,24576]{2,1,0:T(2,128)(2,1)S(1)}, u32[]{:S(2)}, u32[]{:S(2)}) async-start(bf16[4,2,24576]{2,1,0:T(2,128)(2,1)} %reshape.59), calls=%async_computation.1 | async-start | bytes 786432 | tf_op jit(solution)/shard_map/all_to_all | solution.py:33
  99.6 29.6 %all-to-all-start = ((bf16[4,2,24576]{2,1,0:T(2,128)(2,1)}), bf16[4,2,24576]{2,1,0:T(2,128)(2,1)S(1)}, u32[]{:S(2)}, u32[]{:S(2)}) async-start(bf16[4,2,24576]{2,1,0:T(2,128)(2,1)} %reshape.61), calls=%async_computation | async-start | bytes 786432 | tf_op jit(solution)/shard_map/all_to_all | solution.py:34
  103.1 90.8 %all-reduce.3.cloned.1.call-start = ((), (), s32[]{:S(2)}) async-start(), calls=%async_computation.5 | async-start | bytes 3145728 | tf_op jit(solution)/shard_map/psum | solution.py:44
  129.2 20.0 %copy-start.3 = (s32[2,1]{0,1:T(1,128)S(1)}, s32[2,1]{0,1:T(1,128)}, u32[]{:S(2)}) copy-start(s32[2,1]{0,1:T(1,128)} %param.15) | copy-start | bytes 28
  193.9 9.1 %copy-start.4 = (bf16[2,64,2048]{2,1,0:T(8,128)(2,1)S(1)}, bf16[2,64,2048]{2,1,0:T(8,128)(2,1)}, u32[]{:S(2)}) copy-start(bf16[2,64,2048]{2,1,0:T(8,128)(2,1)} %get-tuple-element.5) | copy-start | bytes 1572868
  193.9 9.1 %copy-start.5 = (bf16[2,64,2048]{2,1,0:T(8,128)(2,1)S(1)}, bf16[2,64,2048]{2,1,0:T(8,128)(2,1)}, u32[]{:S(2)}) copy-start(bf16[2,64,2048]{2,1,0:T(8,128)(2,1)} %get-tuple-element.6) | copy-start | bytes 1572868
  203.0 13.5 %copy-start.6 = (bf16[2,64,2048]{2,1,0:T(8,128)(2,1)S(1)}, bf16[2,64,2048]{2,1,0:T(8,128)(2,1)}, u32[]{:S(2)}) copy-start(bf16[2,64,2048]{2,1,0:T(8,128)(2,1)} %get-tuple-element.4) | copy-start | bytes 1572868
  212.7 17.4 %all-to-all-start.2 = ((bf16[2,64,1536]{2,0,1:T(2,128)(2,1)}), bf16[2,64,1536]{2,0,1:T(2,128)(2,1)S(1)}, u32[]{:S(2)}, u32[]{:S(2)}) async-start(bf16[2,64,1536]{2,0,1:T(2,128)(2,1)} %copy.33), calls=%async_computation.2 | async-start | bytes 786432 | tf_op jit(solution)/shard_map/all_to_all | solution.py:66
  216.2 78.8 %reduce-scatter.2.cloned.1.call-start = ((), (), s32[]{:S(2)}) async-start(), calls=%async_computation.4 | async-start | bytes 442368 | tf_op jit(solution)/shard_map/reduce_scatter | solution.py:67
  231.4 63.5 %copy-start.2 = (s32[2,16]{1,0:T(2,128)S(1)}, s32[2,16]{1,0:T(2,128)}, u32[]{:S(2)}) copy-start(s32[2,16]{1,0:T(2,128)} %param.13) | copy-start | bytes 388
  231.4 65.3 %copy-start.1 = (bf16[64,768]{1,0:T(8,128)(2,1)S(1)}, bf16[64,768]{1,0:T(8,128)(2,1)}, u32[]{:S(2)}) copy-start(bf16[64,768]{1,0:T(8,128)(2,1)} %param.8) | copy-start | bytes 294916
Sparse Core Ops, SparseCore 0:
  149.4 44.4 all-reduce.2
  231.6 63.3 reduce-scatter.1
